TPU v7x, 256 devices: a whole 4x4x8 slice. The times are simulated.
256 devices in a mesh: group: 8 (over z), row: 32 (over y, x, core).
Axes of the slice: x: 4, y: 4, z: 8, core: 2. Of those that a mesh axis runs over, the one named last changes fastest.
Arguments:
- start_basis: float32 [2048, 16, 128], P(('group', 'row')), may hold values from -6 to 6
- tiles: bfloat16 [2048, 16, 128, 128], P(('group', 'row')), may hold values from -60000 to 60000
- tile_cols: int32 [2048, 16], P(('group', 'row')), may hold values from 0 to 75, as said below
- tile_count: int32 [2048], P(('group', 'row')), may hold values from 10 to 16, as said below
- recv_list: int32 [8, 32, 32, 2], P('group', 'row'), may hold values from -1 to 2047, as said below
Outputs:
- krylov: float32 [3, 2048, 16, 128], P(None, ('group', 'row'))
Inputs may be any that keep to these rules, and one draw needn't show every extreme that they name: For each reader device and each other device of its range, recv_list names distinct blocks of that peer in its first slots and -1 in the rest; a reader's own entry is all -1; every reader gets exactly 2 blocks from some peer. tile_cols never names an empty receive slot, nor a rim slot of a range that does not exist (before the first or after the last group); every filled receive slot and every existing rim slot is named by some tile slot below 10. `tile_count`: every device has a row block with all 16 tiles live.
All inputs are finite; a program needn't handle non-finite values.
Results may differ from a plain program's by a relative error of at most 0.0003.
Values sent between devices are 32-bit elements; how exact they have to be, the bound alone decides.
A program may use at most 64 MiB of HBM per device.

v0:
```python
import jax
import jax.numpy as jnp
from jax import lax
from jax.sharding import PartitionSpec as P

SLOTS = 2
RIM = 2
ITERS = 3


def padded(x, sides, width):
    for axis, dim in sides:
        count, length = (lax.axis_size(axis), x.shape[dim])
        up = [(i, (i + 1) % count) for i in range(count - 1)]
        down = [(j, i) for i, j in up]
        last = lax.slice_in_dim(x, length - width, length, axis=dim)
        leading = lax.slice_in_dim(x, 0, width, axis=dim)
        before = lax.ppermute(last, axis, up)
        after = lax.ppermute(leading, axis, down)
        x = jnp.concatenate([before, x, after], axis=dim)
    return x


def orthonormal(applied, gram_sum, row_total):
    vectors = applied.shape[1]
    factor = jnp.linalg.cholesky(gram_sum / row_total)
    inverse = lax.linalg.triangular_solve(
        factor, jnp.eye(vectors, dtype=jnp.float32), left_side=True, lower=True
    )
    return jnp.einsum("kl,bli->bki", inverse, applied, precision=lax.Precision.HIGHEST)


def local(start_basis, tiles, tile_cols, tile_count, recv_list):
    groups = lax.axis_size("group")
    peers = lax.axis_size("row")
    group_at = lax.axis_index("group")
    blocks = tiles.shape[0]
    per_row = tiles.shape[1]
    tile_side = tiles.shape[2]
    row_total = groups * peers * blocks * tile_side
    live_mask = (jnp.arange(per_row, dtype=jnp.int32)[None, :] < tile_count[:, None]).astype(
        jnp.float32
    )
    wide_tiles = tiles.astype(jnp.float32)
    sum_sq = jnp.einsum(
        "btij,bt->bi", wide_tiles * wide_tiles, live_mask, precision=lax.Precision.HIGHEST
    )
    inv_root = (1e-06 + sum_sq) ** (-0.25)
    wanted = recv_list.reshape(peers, SLOTS)
    gather_pick = jnp.clip(wanted - group_at * peers * blocks, 0, peers * blocks - 1).reshape(-1)
    results = []
    basis = start_basis
    for step_at in range(ITERS):
        scaled = basis * inv_root[:, None, :]
        rimmed = padded(scaled, (("group", 0),), RIM)
        group_all = lax.all_gather(scaled, "row", axis=0, tiled=True)
        received = jnp.take(group_all, gather_pick, axis=0)
        extended = jnp.concatenate([scaled, received, rimmed[:RIM], rimmed[blocks + RIM :]], axis=0)
        picked = jnp.take(extended, tile_cols, axis=0) * live_mask[:, :, None, None]
        product = jnp.einsum(
            "btij,btkj->bki",
            tiles,
            picked,
            precision=lax.Precision.HIGHEST,
            preferred_element_type=jnp.float32,
        )
        applied = product * inv_root[:, None, :]
        partial_value = jnp.einsum("bki,bli->kl", applied, applied, precision=lax.Precision.HIGHEST)
        gram_sum = lax.psum(partial_value, ("group", "row"))
        basis = orthonormal(applied, gram_sum, row_total)
        results.append(basis)
    return jnp.stack(results)


def solution(mesh):
    placed = (
        P(("group", "row"), None, None),
        P(("group", "row"), None, None, None),
        P(("group", "row"), None),
        P(("group", "row")),
        P("group", "row", None, None),
    )
    return jax.shard_map(
        local,
        mesh=mesh,
        in_specs=placed,
        out_specs=P(None, ("group", "row"), None, None),
        check_vma=False,
    )
```

profile of v0, /device:TPU:1, one launch (start us, length us, event | category | flops | bytes accessed | tf_op | source)
XLA Modules:
  0.0 434.7 jit_solution(10057653734697218750)
XLA Ops:
  6.6 4.5 %multiply_reduce_fusion = f32[8,16,128]{2,1,0:T(8,128)S(1)} fusion(bf16[8,16,128,128]{3,2,1,0:T(8,128)(2,1)} %param.13), kind=kLoop, calls=%fused_computation.6 | loop fusion | flops 6275072 | bytes 4259840 | tf_op jit(solution)/shard_map/btij,bt->bi/reduce_sum | solution.py:45
  12.8 4.4 %collective-permute-start = (f32[2,16,128]{2,1,0:T(8,128)S(1)}, f32[2,16,128]{2,1,0:T(8,128)S(1)}, u32[]{:S(2)}, u32[]{:S(2)}) collective-permute-start(f32[2,16,128]{2,1,0:T(8,128)S(1)} %get-tuple-element.13), channel_id=1, source_target_pairs={{0,32},{32,64},{64,96},{96,128},{128,160},{160,192},{192,224},{1,3... | collective-permute-start | bytes 49160 | tf_op jit(solution)/shard_map/ppermute | solution.py:18
  17.2 1.3 collective-permute-start.1
  18.8 46.4 %all-gather.4.cloned.1.call-done = f32[256,16,128]{2,1,0:T(8,128)} async-done(((f32[8,16,128]{2,1,0:T(8,128)}), f32[256,16,128]{2,1,0:T(8,128)}) %all-gather.4.cloned.1.call-update) | async-done | bytes 2097168 | tf_op jit(solution)/shard_map/all_gather | solution.py:56
  65.2 2.2 gather_fusion
  67.6 0.9 pad_maximum_fusion
  68.5 0.8 gather_fusion.1
  69.2 5.2 %fusion.2 = f32[8,16,128]{2,1,0:T(8,128)S(1)} fusion(bf16[8,16,128,128]{3,2,1,0:T(8,128)(2,1)} %param.13, f32[8,16,16,128]{3,2,1,0:T(8,128)S(1)} %bitcast.92, f32[8,16]{1,0:T(8,128)S(1)} %get-tuple-element.15, pred[8,16]{1,0:T(8,128)(4,1)S(1)} %get-tuple-element.21, f32[8,128]{1,0:T(8,128)S(1)} %add_power_fusion), kind=kOutput, calls=%fused_computation.13 | convolution fusion | flops 403193856 | bytes 5313152 | tf_op jit(solution)/shard_map/btij,btkj->bki/dot_general | solution.py:60
  74.6 75.6 %psum.21 = f32[16,16]{0,1:T(8,128)S(1)} all-reduce(f32[16,16]{0,1:T(8,128)S(1)} %convolution_bitcast_fusion.9), channel_id=1, replica_groups=mesh['group'=8,'row'=32] {'group','row'}, use_global_device_ids=true, to_apply=%region_1.0 | all-reduce | flops 256 | bytes 2048 | tf_op jit(solution)/shard_map/psum | solution.py:69
  150.3 1.5 cholesky.59
  153.0 1.2 custom-call.7
  154.5 0.8 bitcast_multiply_fusion.1
  156.1 2.9 collective-permute-start.2
  159.1 1.3 collective-permute-start.3
  160.4 41.2 %all-gather.6.cloned.1.call-done = f32[256,16,128]{2,1,0:T(8,128)} async-done(((f32[8,16,128]{2,1,0:T(8,128)}), f32[256,16,128]{2,1,0:T(8,128)}) %all-gather.6.cloned.1.call-update) | async-done | bytes 2097168 | tf_op jit(solution)/shard_map/all_gather | solution.py:56
  201.6 2.2 gather_fusion.2
  204.0 0.9 pad_maximum_fusion.1
  204.9 0.8 gather_fusion.3
  205.6 5.2 %fusion.1 = f32[8,16,128]{2,1,0:T(8,128)S(1)} fusion(bf16[8,16,128,128]{3,2,1,0:T(8,128)(2,1)} %param.13, f32[8,16,16,128]{3,2,1,0:T(8,128)S(1)} %bitcast.93, f32[8,16]{1,0:T(8,128)S(1)} %get-tuple-element.15, pred[8,16]{1,0:T(8,128)(4,1)S(1)} %get-tuple-element.21, f32[8,128]{1,0:T(8,128)S(1)} %add_power_fusion), kind=kOutput, calls=%fused_computation.11 | convolution fusion | flops 403193856 | bytes 5313152 | tf_op jit(solution)/shard_map/btij,btkj->bki/dot_general | solution.py:60
  211.0 75.6 %psum.22 = f32[16,16]{0,1:T(8,128)S(1)} all-reduce(f32[16,16]{0,1:T(8,128)S(1)} %convolution_bitcast_fusion.7), channel_id=1, replica_groups=mesh['group'=8,'row'=32] {'group','row'}, use_global_device_ids=true, to_apply=%region_4.9 | all-reduce | flops 256 | bytes 2048 | tf_op jit(solution)/shard_map/psum | solution.py:69
  286.6 1.5 cholesky.70
  289.4 1.2 custom-call.8
  290.9 0.8 bitcast_multiply_fusion
  292.5 2.9 collective-permute-start.4
  295.4 1.3 collective-permute-start.5
  296.7 41.3 %all-gather.8.cloned.1.call-done = f32[256,16,128]{2,1,0:T(8,128)} async-done(((f32[8,16,128]{2,1,0:T(8,128)}), f32[256,16,128]{2,1,0:T(8,128)}) %all-gather.8.cloned.1.call-update) | async-done | bytes 2097168 | tf_op jit(solution)/shard_map/all_gather | solution.py:56
  338.0 2.2 gather_fusion.4
  340.4 0.9 pad_maximum_fusion.2
  342.0 5.2 %fusion = f32[8,16,128]{2,1,0:T(8,128)S(1)} fusion(bf16[8,16,128,128]{3,2,1,0:T(8,128)(2,1)} %param.13, f32[8,16,16,128]{3,2,1,0:T(8,128)S(1)} %bitcast.91, f32[8,16]{1,0:T(8,128)S(1)} %get-tuple-element.15, pred[8,16]{1,0:T(8,128)(4,1)S(1)} %get-tuple-element.21, f32[8,128]{1,0:T(8,128)S(1)} %add_power_fusion), kind=kOutput, calls=%fused_computation.9 | convolution fusion | flops 403193856 | bytes 5313152 | tf_op jit(solution)/shard_map/btij,btkj->bki/dot_general | solution.py:60
  347.4 75.6 %psum.23 = f32[16,16]{0,1:T(8,128)S(1)} all-reduce(f32[16,16]{0,1:T(8,128)S(1)} %convolution_bitcast_fusion.5), channel_id=1, replica_groups=mesh['group'=8,'row'=32] {'group','row'}, use_global_device_ids=true, to_apply=%region_5.10 | all-reduce | flops 256 | bytes 2048 | tf_op jit(solution)/shard_map/psum | solution.py:69
  423.0 1.5 cholesky.81
  425.8 1.2 custom-call.9
  (66 shorter events, 11.1 us)
Async XLA Ops:
  6.5 4.5 %copy-start.1 = (s32[8,16]{1,0:T(8,128)S(1)}, s32[8,16]{1,0:T(8,128)}, u32[]{:S(2)}) copy-start(s32[8,16]{1,0:T(8,128)} %param.14) | copy-start | bytes 1540
  6.5 4.5 %copy-start.3 = (s32[8]{0:T(128)S(1)}, s32[8]{0:T(128)}, u32[]{:S(2)}) copy-start(s32[8]{0:T(128)} %param.15) | copy-start | bytes 100
  6.5 4.8 %copy-start = (f32[8,16,128]{2,1,0:T(8,128)S(1)}, f32[8,16,128]{2,1,0:T(8,128)}, u32[]{:S(2)}) copy-start(f32[8,16,128]{2,1,0:T(8,128)} %param.12) | copy-start | bytes 196612
  6.5 12.0 %copy-start.2 = (s32[1,1,32,2]{2,3,1,0:T(2,128)S(1)}, s32[1,1,32,2]{2,3,1,0:T(2,128)}, u32[]{:S(2)}) copy-start(s32[1,1,32,2]{2,3,1,0:T(2,128)} %param.16) | copy-start | bytes 772
  6.5 58.7 %all-gather.4.cloned.1.call-start = ((), (), s32[]{:S(2)}) async-start(), calls=%async_computation | async-start | bytes 2162688 | tf_op jit(solution)/shard_map/all_gather | solution.py:56
  12.0 189.6 %all-gather.6.cloned.1.call-start = ((), (), s32[]{:S(2)}) async-start(), calls=%async_computation.1 | async-start | bytes 2162688 | tf_op jit(solution)/shard_map/all_gather | solution.py:56
  12.8 54.8 %collective-permute-start = (f32[2,16,128]{2,1,0:T(8,128)S(1)}, f32[2,16,128]{2,1,0:T(8,128)S(1)}, u32[]{:S(2)}, u32[]{:S(2)}) collective-permute-start(f32[2,16,128]{2,1,0:T(8,128)S(1)} %get-tuple-element.13), channel_id=1, source_target_pairs={{0,32},{32,64},{64,96},{96,128},{128,160},{160,192},{192,224},{1,3... | collective-permute-start | bytes 49160 | tf_op jit(solution)/shard_map/ppermute | solution.py:18
  17.2 50.4 %collective-permute-start.1 = (f32[2,16,128]{2,1,0:T(8,128)S(1)}, f32[2,16,128]{2,1,0:T(8,128)S(1)}, u32[]{:S(2)}, u32[]{:S(2)}) collective-permute-start(f32[2,16,128]{2,1,0:T(8,128)S(1)} %get-tuple-element.14), channel_id=1, source_target_pairs={{32,0},{64,32},{96,64},{128,96},{160,128},{192,160},{224,192},{33,... | collective-permute-start | bytes 49160 | tf_op jit(solution)/shard_map/ppermute | solution.py:19
  155.3 182.7 %all-gather.8.cloned.1.call-start = ((), (), s32[]{:S(2)}) async-start(), calls=%async_computation.2 | async-start | bytes 2162688 | tf_op jit(solution)/shard_map/all_gather | solution.py:56
  156.1 47.8 %collective-permute-start.2 = (f32[2,16,128]{2,1,0:T(8,128)S(1)}, f32[2,16,128]{2,1,0:T(8,128)S(1)}, u32[]{:S(2)}, u32[]{:S(2)}) collective-permute-start(f32[2,16,128]{2,1,0:T(8,128)S(1)} %get-tuple-element.10), channel_id=1, source_target_pairs={{0,32},{32,64},{64,96},{96,128},{128,160},{160,192},{192,224},{1,3... | collective-permute-start | bytes 49160 | tf_op jit(solution)/shard_map/ppermute | solution.py:18
  159.1 44.9 %collective-permute-start.3 = (f32[2,16,128]{2,1,0:T(8,128)S(1)}, f32[2,16,128]{2,1,0:T(8,128)S(1)}, u32[]{:S(2)}, u32[]{:S(2)}) collective-permute-start(f32[2,16,128]{2,1,0:T(8,128)S(1)} %get-tuple-element.12), channel_id=1, source_target_pairs={{32,0},{64,32},{96,64},{128,96},{160,128},{192,160},{224,192},{33,... | collective-permute-start | bytes 49160 | tf_op jit(solution)/shard_map/ppermute | solution.py:19
  292.5 47.9 %collective-permute-start.4 = (f32[2,16,128]{2,1,0:T(8,128)S(1)}, f32[2,16,128]{2,1,0:T(8,128)S(1)}, u32[]{:S(2)}, u32[]{:S(2)}) collective-permute-start(f32[2,16,128]{2,1,0:T(8,128)S(1)} %get-tuple-element.6), channel_id=1, source_target_pairs={{0,32},{32,64},{64,96},{96,128},{128,160},{160,192},{192,224},{1,3... | collective-permute-start | bytes 49160 | tf_op jit(solution)/shard_map/ppermute | solution.py:18
  295.4 44.9 %collective-permute-start.5 = (f32[2,16,128]{2,1,0:T(8,128)S(1)}, f32[2,16,128]{2,1,0:T(8,128)S(1)}, u32[]{:S(2)}, u32[]{:S(2)}) collective-permute-start(f32[2,16,128]{2,1,0:T(8,128)S(1)} %get-tuple-element.8), channel_id=1, source_target_pairs={{32,0},{64,32},{96,64},{128,96},{160,128},{192,160},{224,192},{33,... | collective-permute-start | bytes 49160 | tf_op jit(solution)/shard_map/ppermute | solution.py:19
Sparse Core Ops, SparseCore 0:
  12.1 53.0 all-gather.3
  155.5 46.1 all-gather.5
  291.8 46.1 all-gather.7
where the time goes:
time: 436 us; the launch traced here: 435 us
  blocking collectives  227 us (52%)
  waiting for transfers between devices  129 us (30%)
  other arithmetic  21 us (5%)
  matrix products  18.7 us (4%)
  starting transfers between devices  14.2 us (3%)
  between operations  13.4 us (3%)
  local copies, waits for them, and re-layouts  11.6 us (3%)
    psum x3, blocking collectives, local(): gram_sum = lax.psum(partial_value, ('group', 'row'))  227 us
    all_gather x3, waiting for transfers between devices, local(): group_all = lax.all_gather(scaled, 'row', axis=0, tiled=True)  129 us
    dot_general x3, matrix products, local(): jnp.einsum('btij,btkj->bki', tiles, picked, precision=lax.Precision.HIGHE...  15.5 us
    ppermute x3, starting transfers between devices, padded(): before = lax.ppermute(last, axis, up)  10.2 us
  transfers between devices with their start and end apart: 9, of which 3 were waited for; matrix products, arithmetic and copies ran while one was open for 2% of the time, Pallas kernels for 0%

commit v1 on v0

--- a/solution.py
+++ b/solution.py
@@ -66,7 +66,7 @@
         )
         applied = product * inv_root[:, None, :]
         partial_value = jnp.einsum("bki,bli->kl", applied, applied, precision=lax.Precision.HIGHEST)
-        gram_sum = lax.psum(partial_value, ("group", "row"))
+        gram_sum = jnp.sum(lax.all_gather(partial_value, ("group", "row")), axis=0)
         basis = orthonormal(applied, gram_sum, row_total)
         results.append(basis)
     return jnp.stack(results)

time: 436 us -> 416 us (0.954)
  blocking collectives: 227 us -> 207 us
    psum x3 -> x0, blocking collectives: 227 us -> none  [local(): gram_sum = lax.psum(partial_value, ('group', 'row'))]
    all_gather x0 -> x3, blocking collectives: none -> 207 us  [local(): gram_sum = jnp.sum(lax.all_gather(partial_value, ('group', 'row')), axis=0)]
where the time goes in v1:
time: 416 us; the launch traced here: 415 us
  blocking collectives  207 us (50%)
  waiting for transfers between devices  129 us (31%)
  other arithmetic  21.9 us (5%)
  matrix products  18.7 us (4%)
  starting transfers between devices  13.4 us (3%)
  between operations  13.4 us (3%)
  local copies, waits for them, and re-layouts  11.8 us (3%)
    all_gather x3, blocking collectives, local(): gram_sum = jnp.sum(lax.all_gather(partial_value, ('group', 'row')), axis=0)  207 us
    all_gather x3, waiting for transfers between devices, local(): group_all = lax.all_gather(scaled, 'row', axis=0, tiled=True)  129 us
    dot_general x3, matrix products, local(): jnp.einsum('btij,btkj->bki', tiles, picked, precision=lax.Precision.HIGHE...  15.5 us
    ppermute x3, starting transfers between devices, padded(): before = lax.ppermute(last, axis, up)  9.46 us
  transfers between devices with their start and end apart: 9, of which 3 were waited for; matrix products, arithmetic and copies ran while one was open for 2% of the time, Pallas kernels for 0%

profile of v1, /device:TPU:1, one launch (start us, length us, event | category | flops | bytes accessed | tf_op | source)
XLA Modules:
  0.0 414.7 jit_solution(14175272219558175602)
XLA Ops:
  6.6 4.5 %multiply_reduce_fusion = f32[8,16,128]{2,1,0:T(8,128)S(1)} fusion(bf16[8,16,128,128]{3,2,1,0:T(8,128)(2,1)} %param.13), kind=kLoop, calls=%fused_computation.6 | loop fusion | flops 6275072 | bytes 4259840 | tf_op jit(solution)/shard_map/btij,bt->bi/reduce_sum | solution.py:45
  12.8 4.4 %collective-permute-start = (f32[2,16,128]{2,1,0:T(8,128)S(1)}, f32[2,16,128]{2,1,0:T(8,128)S(1)}, u32[]{:S(2)}, u32[]{:S(2)}) collective-permute-start(f32[2,16,128]{2,1,0:T(8,128)S(1)} %get-tuple-element.13), channel_id=1, source_target_pairs={{0,32},{32,64},{64,96},{96,128},{128,160},{160,192},{192,224},{1,3... | collective-permute-start | bytes 49160 | tf_op jit(solution)/shard_map/ppermute | solution.py:18
  17.2 1.3 collective-permute-start.1
  18.8 46.4 %all-gather.7.cloned.1.call-done = f32[256,16,128]{2,1,0:T(8,128)} async-done(((f32[8,16,128]{2,1,0:T(8,128)}), f32[256,16,128]{2,1,0:T(8,128)}) %all-gather.7.cloned.1.call-update) | async-done | bytes 2097168 | tf_op jit(solution)/shard_map/all_gather | solution.py:56
  65.2 2.2 gather_fusion
  67.6 0.9 pad_maximum_fusion
  68.5 0.8 gather_fusion.1
  69.2 5.2 %fusion.2 = f32[8,16,128]{2,1,0:T(8,128)S(1)} fusion(bf16[8,16,128,128]{3,2,1,0:T(8,128)(2,1)} %param.13, f32[8,16,16,128]{3,2,1,0:T(8,128)S(1)} %bitcast.98, f32[8,16]{1,0:T(8,128)S(1)} %get-tuple-element.15, pred[8,16]{1,0:T(8,128)(4,1)S(1)} %get-tuple-element.21, f32[8,128]{1,0:T(8,128)S(1)} %add_power_fusion), kind=kOutput, calls=%fused_computation.13 | convolution fusion | flops 403193856 | bytes 5313152 | tf_op jit(solution)/shard_map/btij,btkj->bki/dot_general | solution.py:60
  74.6 68.8 %all-gather = f32[4096,16]{1,0:T(8,128)S(1)} all-gather(f32[16,16]{1,0:T(8,128)S(1)} %convolution_bitcast_fusion.9), channel_id=2, replica_groups=mesh['group'=8,'row'=32] {'group','row'}, dimensions={0}, use_global_device_ids=true | all-gather | bytes 263168 | tf_op jit(solution)/shard_map/all_gather | solution.py:69
  143.9 1.5 cholesky.59
  146.7 1.2 custom-call.7
  148.1 0.8 bitcast_multiply_fusion.1
  149.7 2.5 collective-permute-start.2
  152.3 1.3 collective-permute-start.3
  153.6 41.1 %all-gather.9.cloned.1.call-done = f32[256,16,128]{2,1,0:T(8,128)} async-done(((f32[8,16,128]{2,1,0:T(8,128)}), f32[256,16,128]{2,1,0:T(8,128)}) %all-gather.9.cloned.1.call-update) | async-done | bytes 2097168 | tf_op jit(solution)/shard_map/all_gather | solution.py:56
  194.7 2.2 gather_fusion.2
  197.1 0.9 pad_maximum_fusion.1
  198.0 0.8 gather_fusion.3
  198.8 5.2 %fusion.1 = f32[8,16,128]{2,1,0:T(8,128)S(1)} fusion(bf16[8,16,128,128]{3,2,1,0:T(8,128)(2,1)} %param.13, f32[8,16,16,128]{3,2,1,0:T(8,128)S(1)} %bitcast.99, f32[8,16]{1,0:T(8,128)S(1)} %get-tuple-element.15, pred[8,16]{1,0:T(8,128)(4,1)S(1)} %get-tuple-element.21, f32[8,128]{1,0:T(8,128)S(1)} %add_power_fusion), kind=kOutput, calls=%fused_computation.11 | convolution fusion | flops 403193856 | bytes 5313152 | tf_op jit(solution)/shard_map/btij,btkj->bki/dot_general | solution.py:60
  204.1 69.0 %all-gather.1 = f32[4096,16]{1,0:T(8,128)S(1)} all-gather(f32[16,16]{1,0:T(8,128)S(1)} %convolution_bitcast_fusion.7), channel_id=3, replica_groups=mesh['group'=8,'row'=32] {'group','row'}, dimensions={0}, use_global_device_ids=true | all-gather | bytes 263168 | tf_op jit(solution)/shard_map/all_gather | solution.py:69
  273.6 1.5 cholesky.70
  276.3 1.2 custom-call.8
  277.8 0.8 bitcast_multiply_fusion
  279.4 2.5 collective-permute-start.4
  281.9 1.3 collective-permute-start.5
  283.2 41.2 %all-gather.11.cloned.1.call-done = f32[256,16,128]{2,1,0:T(8,128)} async-done(((f32[8,16,128]{2,1,0:T(8,128)}), f32[256,16,128]{2,1,0:T(8,128)}) %all-gather.11.cloned.1.call-update) | async-done | bytes 2097168 | tf_op jit(solution)/shard_map/all_gather | solution.py:56
  324.4 2.2 gather_fusion.4
  326.8 0.9 pad_maximum_fusion.2
  328.4 5.2 %fusion = f32[8,16,128]{2,1,0:T(8,128)S(1)} fusion(bf16[8,16,128,128]{3,2,1,0:T(8,128)(2,1)} %param.13, f32[8,16,16,128]{3,2,1,0:T(8,128)S(1)} %bitcast.97, f32[8,16]{1,0:T(8,128)S(1)} %get-tuple-element.15, pred[8,16]{1,0:T(8,128)(4,1)S(1)} %get-tuple-element.21, f32[8,128]{1,0:T(8,128)S(1)} %add_power_fusion), kind=kOutput, calls=%fused_computation.9 | convolution fusion | flops 403193856 | bytes 5313152 | tf_op jit(solution)/shard_map/btij,btkj->bki/dot_general | solution.py:60
  333.8 68.8 %all-gather.2 = f32[4096,16]{1,0:T(8,128)S(1)} all-gather(f32[16,16]{1,0:T(8,128)S(1)} %convolution_bitcast_fusion.5), channel_id=4, replica_groups=mesh['group'=8,'row'=32] {'group','row'}, dimensions={0}, use_global_device_ids=true | all-gather | bytes 263168 | tf_op jit(solution)/shard_map/all_gather | solution.py:69
  403.1 1.5 cholesky.81
  405.9 1.2 custom-call.9
  (72 shorter events, 12.1 us)
Async XLA Ops:
  6.5 4.5 %copy-start.1 = (s32[8,16]{1,0:T(8,128)S(1)}, s32[8,16]{1,0:T(8,128)}, u32[]{:S(2)}) copy-start(s32[8,16]{1,0:T(8,128)} %param.14) | copy-start | bytes 1540
  6.5 4.5 %copy-start.3 = (s32[8]{0:T(128)S(1)}, s32[8]{0:T(128)}, u32[]{:S(2)}) copy-start(s32[8]{0:T(128)} %param.15) | copy-start | bytes 100
  6.5 4.8 %copy-start = (f32[8,16,128]{2,1,0:T(8,128)S(1)}, f32[8,16,128]{2,1,0:T(8,128)}, u32[]{:S(2)}) copy-start(f32[8,16,128]{2,1,0:T(8,128)} %param.12) | copy-start | bytes 196612
  6.5 12.0 %copy-start.2 = (s32[1,1,32,2]{2,3,1,0:T(2,128)S(1)}, s32[1,1,32,2]{2,3,1,0:T(2,128)}, u32[]{:S(2)}) copy-start(s32[1,1,32,2]{2,3,1,0:T(2,128)} %param.16) | copy-start | bytes 772
  6.5 58.7 %all-gather.7.cloned.1.call-start = ((), (), s32[]{:S(2)}) async-start(), calls=%async_computation | async-start | bytes 2162688 | tf_op jit(solution)/shard_map/all_gather | solution.py:56
  12.0 182.8 %all-gather.9.cloned.1.call-start = ((), (), s32[]{:S(2)}) async-start(), calls=%async_computation.1 | async-start | bytes 2162688 | tf_op jit(solution)/shard_map/all_gather | solution.py:56
  12.8 54.8 %collective-permute-start = (f32[2,16,128]{2,1,0:T(8,128)S(1)}, f32[2,16,128]{2,1,0:T(8,128)S(1)}, u32[]{:S(2)}, u32[]{:S(2)}) collective-permute-start(f32[2,16,128]{2,1,0:T(8,128)S(1)} %get-tuple-element.13), channel_id=1, source_target_pairs={{0,32},{32,64},{64,96},{96,128},{128,160},{160,192},{192,224},{1,3... | collective-permute-start | bytes 49160 | tf_op jit(solution)/shard_map/ppermute | solution.py:18
  17.2 50.4 %collective-permute-start.1 = (f32[2,16,128]{2,1,0:T(8,128)S(1)}, f32[2,16,128]{2,1,0:T(8,128)S(1)}, u32[]{:S(2)}, u32[]{:S(2)}) collective-permute-start(f32[2,16,128]{2,1,0:T(8,128)S(1)} %get-tuple-element.14), channel_id=1, source_target_pairs={{32,0},{64,32},{96,64},{128,96},{160,128},{192,160},{224,192},{33,... | collective-permute-start | bytes 49160 | tf_op jit(solution)/shard_map/ppermute | solution.py:19
  149.0 175.5 %all-gather.11.cloned.1.call-start = ((), (), s32[]{:S(2)}) async-start(), calls=%async_computation.2 | async-start | bytes 2162688 | tf_op jit(solution)/shard_map/all_gather | solution.py:56
  149.7 47.3 %collective-permute-start.2 = (f32[2,16,128]{2,1,0:T(8,128)S(1)}, f32[2,16,128]{2,1,0:T(8,128)S(1)}, u32[]{:S(2)}, u32[]{:S(2)}) collective-permute-start(f32[2,16,128]{2,1,0:T(8,128)S(1)} %get-tuple-element.10), channel_id=1, source_target_pairs={{0,32},{32,64},{64,96},{96,128},{128,160},{160,192},{192,224},{1,3... | collective-permute-start | bytes 49160 | tf_op jit(solution)/shard_map/ppermute | solution.py:18
  152.3 44.8 %collective-permute-start.3 = (f32[2,16,128]{2,1,0:T(8,128)S(1)}, f32[2,16,128]{2,1,0:T(8,128)S(1)}, u32[]{:S(2)}, u32[]{:S(2)}) collective-permute-start(f32[2,16,128]{2,1,0:T(8,128)S(1)} %get-tuple-element.12), channel_id=1, source_target_pairs={{32,0},{64,32},{96,64},{128,96},{160,128},{192,160},{224,192},{33,... | collective-permute-start | bytes 49160 | tf_op jit(solution)/shard_map/ppermute | solution.py:19
  279.4 47.4 %collective-permute-start.4 = (f32[2,16,128]{2,1,0:T(8,128)S(1)}, f32[2,16,128]{2,1,0:T(8,128)S(1)}, u32[]{:S(2)}, u32[]{:S(2)}) collective-permute-start(f32[2,16,128]{2,1,0:T(8,128)S(1)} %get-tuple-element.6), channel_id=1, source_target_pairs={{0,32},{32,64},{64,96},{96,128},{128,160},{160,192},{192,224},{1,3... | collective-permute-start | bytes 49160 | tf_op jit(solution)/shard_map/ppermute | solution.py:18
  281.9 44.8 %collective-permute-start.5 = (f32[2,16,128]{2,1,0:T(8,128)S(1)}, f32[2,16,128]{2,1,0:T(8,128)S(1)}, u32[]{:S(2)}, u32[]{:S(2)}) collective-permute-start(f32[2,16,128]{2,1,0:T(8,128)S(1)} %get-tuple-element.8), channel_id=1, source_target_pairs={{32,0},{64,32},{96,64},{128,96},{160,128},{192,160},{224,192},{33,... | collective-permute-start | bytes 49160 | tf_op jit(solution)/shard_map/ppermute | solution.py:19
Sparse Core Ops, SparseCore 0:
  12.1 53.0 all-gather.6
  149.1 45.6 all-gather.8
  278.8 45.6 all-gather.10
